TPU v7x, 32 devices: a whole 2x2x4 slice. The times are simulated.
32 devices in a mesh: gx: 4 (over y, x), gy: 4 (over z), gz: 2 (over core).
Axes of the slice: x: 2, y: 2, z: 4, core: 2. Of those that a mesh axis runs over, the one named last changes fastest.
Arguments:
- position: float32 [4096, 3, 128], P(('gx', 'gy', 'gz')), may hold values from 0 to 4, as said below
- velocity: float32 [4096, 3, 128], P(('gx', 'gy', 'gz')), may hold values from -0.3 to 0.3
- particle_mass: float32 [4096, 128], P(('gx', 'gy', 'gz')), may hold values from 0.001953125 to 0.0078125
- send_first: int32 [32, 32, 4], P(('gx', 'gy', 'gz')), may hold values from -1 to 127, as said below
- neighbours_first: int32 [4096, 16], P(('gx', 'gy', 'gz')), may hold values from 0 to 255, as said below
- destination: int32 [4096], P(('gx', 'gy', 'gz')), may hold values from 0 to 4095, as said below
- send_second: int32 [32, 32, 4], P(('gx', 'gy', 'gz')), may hold values from -1 to 127, as said below
- neighbours_second: int32 [4096, 16], P(('gx', 'gy', 'gz')), may hold values from 0 to 255, as said below
Outputs:
- position_out: float32 [4096, 3, 128], P(('gx', 'gy', 'gz'))
- velocity_out: float32 [4096, 3, 128], P(('gx', 'gy', 'gz'))
- density_out: float32 [4096, 128], P(('gx', 'gy', 'gz'))
Inputs may be any that keep to these rules, and one draw needn't show every extreme that they name: The particles of a block owned by the device at grid position (i_gx, i_gy, i_gz) lie in its box [i_gx, i_gx + 1] x [i_gy, i_gy + 1] x [i_gz, i_gz + 1], all of one block within a cube of side 1/2. `send_first`: only devices whose grid positions along gx, gy and gz differ by at most one in each (and are not the same) send ghosts to each other. The filled slots of one pair come first and hold distinct blocks; some pair fills all 4 slots. `send_second`: as for send_first, in the new layout. `neighbours_first`: entries name only the device's own blocks or filled ghost slots of send_first; the entries of a block are distinct and never the block itself. `neighbours_second`: entries name only the device's own blocks or filled ghost slots of send_second; the entries of a block are distinct and never the block itself. `destination`: A permutation of the 4096 positions; a block stays or moves to a device next to its owner along exactly one of gx, gy, gz; at most 2 blocks go from one device to another, and some pairs move exactly 2.
All inputs are finite; a program needn't handle non-finite values.
Results may differ from a plain program's by a relative error of at most 0.0001.
Values sent between devices are 32-bit elements; how exact they have to be, the bound alone decides.
A program may use at most 128 MiB of HBM per device.

v0:
```python
import jax
import jax.numpy as jnp
import numpy as np
from jax import lax
from jax.sharding import PartitionSpec as P

MOVE_CAP = 2


smooth_len = 0.5
time_step = 0.25
column_group = 4


def padded_2(block, sides, width):
    for axis, dim in sides:
        count = lax.axis_size(axis)
        forward = [(i, i + 1) for i in range(count - 1)]
        backward = [(target, source) for source, target in forward]
        low = lax.ppermute(
            lax.slice_in_dim(block, block.shape[dim] - width, None, axis=dim), axis, forward
        )
        high = lax.ppermute(lax.slice_in_dim(block, 0, width, axis=dim), axis, backward)
        block = jnp.concatenate([low, block, high], axis=dim)
    return block


def pair_density(home_points, away_points, away_mass):
    offset = home_points[:, :, :, None] - away_points[:, :, None, :]
    squared = jnp.sum(offset * offset, axis=1)
    kernel = jnp.maximum(1.0 - squared / (smooth_len * smooth_len), 0.0)
    return jnp.sum(away_mass[:, None, :] * (kernel * kernel * kernel), axis=2)


def pair_force(home_points, home_term, away_points, away_mass, away_term):
    offset = home_points[:, :, :, None] - away_points[:, :, None, :]
    squared = jnp.sum(offset * offset, axis=1)
    kernel = jnp.maximum(1.0 - squared / (smooth_len * smooth_len), 0.0)
    weight = (
        away_mass[:, None, :] * (home_term[:, :, None] + away_term[:, None, :]) * kernel * kernel
    )
    return 6.0 / (smooth_len * smooth_len) * jnp.sum(weight[:, None, :, :] * offset, axis=3)


def pressure_term(density):
    return jnp.exp(jnp.log(density) * (-1.0 / 3.0))


def joined_points(all_points, picked):
    chosen = all_points[picked]
    rows = chosen.shape[0]
    return jnp.transpose(chosen, (0, 2, 1, 3)).reshape(
        rows, chosen.shape[2], chosen.shape[1] * chosen.shape[3]
    )


def joined_values(all_values, picked):
    chosen = all_values[picked]
    return chosen.reshape(chosen.shape[0], chosen.shape[1] * chosen.shape[2])


def table_density(home_points, home_mass, all_points, all_mass, lookup):
    initial = pair_density(home_points, home_points, home_mass)

    def add_group(group, running):
        picked = lax.dynamic_slice_in_dim(lookup, group * column_group, column_group, 1)
        return running + pair_density(
            home_points, joined_points(all_points, picked), joined_values(all_mass, picked)
        )

    return lax.fori_loop(0, lookup.shape[1] // column_group, add_group, initial)


def table_force(home_points, home_mass, home_term, all_points, all_mass, all_term, lookup):
    initial = pair_force(home_points, home_term, home_points, home_mass, home_term)

    def add_group(group, running):
        picked = lax.dynamic_slice_in_dim(lookup, group * column_group, column_group, 1)
        return running + pair_force(
            home_points,
            home_term,
            joined_points(all_points, picked),
            joined_values(all_mass, picked),
            joined_values(all_term, picked),
        )

    return lax.fori_loop(0, lookup.shape[1] // column_group, add_group, initial)


def near_slots(sender_rows):
    size_x = lax.axis_size("gx")
    size_y = lax.axis_size("gy")
    size_z = lax.axis_size("gz")
    shifts = np.array(
        [
            [first, second, third]
            for first in (-1, 0, 1)
            for second in (-1, 0, 1)
            for third in (-1, 0, 1)
        ],
        dtype=np.int32,
    )
    target_x = lax.axis_index("gx") + shifts[:, 0]
    target_y = lax.axis_index("gy") + shifts[:, 1]
    target_z = lax.axis_index("gz") + shifts[:, 2]
    inside = (target_x >= 0) & (target_x < size_x) & (target_y >= 0) & (target_y < size_y)
    inside = inside & (target_z >= 0) & (target_z < size_z)
    target = (target_x * size_y + target_y) * size_z + target_z
    picked = sender_rows[jnp.clip(target, 0, sender_rows.shape[0] - 1)]
    return jnp.where(inside[:, None], picked, -1)


def fill_slots(payload, sender_rows, blank):
    usable = sender_rows >= 0
    gathered = payload[jnp.maximum(sender_rows, 0)]
    broadcast_shape = usable.shape + (1,) * (payload.ndim - 1)
    return jnp.where(usable.reshape(broadcast_shape), gathered, blank)


def ghost_blocks(payload, sender_rows):
    buffer = fill_slots(payload, near_slots(sender_rows), 0.0)
    cube = buffer.reshape((3, 3, 3) + buffer.shape[1:])
    padded = padded_2(cube, (("gx", 0), ("gy", 1), ("gz", 2)), 1)
    return padded[0::2, 0::2, 0::2].reshape((-1,) + payload.shape[1:])


def ghost_density(density, sender_rows):
    buffer = fill_slots(density, near_slots(sender_rows), 1.0)
    cube = buffer.reshape((3, 3, 3) + buffer.shape[1:])
    padded = padded_2(cube, (("gx", 0), ("gy", 1), ("gz", 2)), 1)
    return padded[0::2, 0::2, 0::2].reshape((-1,) + density.shape[1:])


def table_rows(neighbours, blocks, ghost_cap):
    size_y = lax.axis_size("gy")
    size_z = lax.axis_size("gz")
    remote = jnp.maximum(neighbours - blocks, 0)
    source = remote // ghost_cap
    within = remote % ghost_cap
    code = (source // (size_y * size_z) - lax.axis_index("gx") + 1) * 9
    code = code + (source // size_z % size_y - lax.axis_index("gy") + 1) * 3
    code = code + (source % size_z - lax.axis_index("gz") + 1)
    return jnp.where(neighbours < blocks, neighbours, blocks + code * ghost_cap + within)


def sph_forces(points, weights, sender_rows, neighbours):
    blocks = points.shape[0]
    payload = jnp.concatenate([points, weights[:, None, :]], axis=1)
    stacked = jnp.concatenate([payload, ghost_blocks(payload, sender_rows)], axis=0)
    lookup = table_rows(neighbours, blocks, sender_rows.shape[1])
    all_points = stacked[:, 0:3]
    all_mass = stacked[:, 3]
    density = table_density(points, weights, all_points, all_mass, lookup)
    all_rho = jnp.concatenate([density, ghost_density(density, sender_rows)], axis=0)
    all_term = pressure_term(all_rho)
    acceleration = table_force(
        points, weights, all_term[:blocks], all_points, all_mass, all_term, lookup
    )
    return (density, acceleration)


def migrate(fields, destination):
    blocks = fields.shape[0]
    width = fields.shape[2]
    myself = lax.axis_index(("gx", "gy", "gz"))
    owner_device = destination // blocks
    new_place = destination % blocks
    moving = owner_device != myself
    label_row = (
        jnp.zeros((blocks, 1, width), jnp.float32)
        .at[:, 0, 0]
        .set((new_place + 1).astype(jnp.float32))
    )
    carried = jnp.concatenate([fields, label_row], axis=1)
    staying = (
        jnp.zeros_like(fields).at[jnp.where(moving, blocks, new_place)].set(fields, mode="drop")
    )
    size_y = lax.axis_size("gy")
    size_z = lax.axis_size("gz")
    delta_x = owner_device // (size_y * size_z) - lax.axis_index("gx")
    delta_y = owner_device // size_z % size_y - lax.axis_index("gy")
    delta_z = owner_device % size_z - lax.axis_index("gz")
    heading = jnp.where(
        delta_x != 0,
        (delta_x > 0).astype(jnp.int32),
        jnp.where(
            delta_y != 0, 2 + (delta_y > 0).astype(jnp.int32), 4 + (delta_z > 0).astype(jnp.int32)
        ),
    )
    bin_count = 6
    onehot = (
        (heading[:, None] == jnp.arange(bin_count, dtype=jnp.int32)[None, :]) & moving[:, None]
    ).astype(jnp.int32)
    earlier = jnp.sum((jnp.cumsum(onehot, axis=0) - onehot) * onehot, axis=1)
    outbox_slot = jnp.where(moving, heading * MOVE_CAP + earlier, bin_count * MOVE_CAP)
    outbox = (
        jnp.zeros((bin_count * MOVE_CAP,) + carried.shape[1:], jnp.float32)
        .at[outbox_slot]
        .set(carried, mode="drop")
    )
    outbound = outbox.reshape((3, 2, MOVE_CAP) + carried.shape[1:])
    came_x = padded_2(outbound[0], (("gx", 0),), 1)
    came_y = padded_2(outbound[1], (("gy", 0),), 1)
    came_z = padded_2(outbound[2], (("gz", 0),), 1)
    arrived = jnp.concatenate(
        [came_x[0], came_x[3], came_y[0], came_y[3], came_z[0], came_z[3]], axis=0
    )
    labels = arrived[:, 7, 0]
    arrive_place = jnp.where(labels > 0.5, labels.astype(jnp.int32) - 1, blocks)
    return staying.at[arrive_place].set(arrived[:, 0:7], mode="drop")


def per_device(
    position,
    velocity,
    particle_mass,
    send_first,
    neighbours_first,
    destination,
    send_second,
    neighbours_second,
):
    density, acceleration = sph_forces(position, particle_mass, send_first[0], neighbours_first)
    velocity = velocity + time_step * acceleration
    position = position + time_step * velocity
    fields = jnp.concatenate([position, velocity, particle_mass[:, None, :]], axis=1)
    shifted = migrate(fields, destination)
    position = shifted[:, 0:3]
    velocity = shifted[:, 3:6]
    moved_mass = shifted[:, 6]
    density, acceleration = sph_forces(position, moved_mass, send_second[0], neighbours_second)
    velocity = velocity + time_step * acceleration
    position = position + time_step * velocity
    return (position, velocity, density)


def solution(mesh):
    in_specs = (
        P(("gx", "gy", "gz"), None, None),
        P(("gx", "gy", "gz"), None, None),
        P(("gx", "gy", "gz"), None),
        P(("gx", "gy", "gz"), None, None),
        P(("gx", "gy", "gz"), None),
        P(("gx", "gy", "gz")),
        P(("gx", "gy", "gz"), None, None),
        P(("gx", "gy", "gz"), None),
    )
    out_specs = (
        P(("gx", "gy", "gz"), None, None),
        P(("gx", "gy", "gz"), None, None),
        P(("gx", "gy", "gz"), None),
    )
    return jax.shard_map(
        per_device, mesh=mesh, in_specs=in_specs, out_specs=out_specs, check_vma=False
    )
```

profile of v0, /device:TPU:0, one launch (start us, length us, event | category | flops | bytes accessed | tf_op | source)
XLA Modules:
  0.0 1248.9 jit_solution(4794121178652074883)
XLA Ops:
  16.0 11.5 fusion.8
  53.0 187.7 %while.53 = (s32[]{:T(128)}, f32[128,128]{1,0:T(8,128)S(1)}, s32[128,16]{1,0:T(8,128)S(1)}, f32[236,128]{1,0:T(8,128)S(1)}, f32[128,3,128]{2,1,0:T(4,128)S(1)}, ...) while((s32[]{:T(128)}, f32[128,128]{1,0:T(8,128)S(1)}, ...), condition=%wide.region_5.6_spmd, body=%wide.region_2.5_spmd.sunk | while | flops 125831688 | bytes 71256216 | solution.py:71
  55.3 28.7 %multiply_reduce_fusion.4 = f32[128,128,512]{2,1,0:T(8,128)} fusion(f32[128,3,512]{2,1,0:T(4,128)S(1)} %bitcast.105, f32[128,3,128]{2,1,0:T(4,128)S(1)} %get-tuple-element.882), kind=kLoop, calls=%fused_computation.19.clone.1 | loop fusion | flops 67108864 | bytes 34537472 | tf_op jit(solution)/shard_map/while/body/eval_jaxpr/reduce_sum | solution.py:30
  85.1 14.8 %fusion.79 = f32[128,128]{1,0:T(8,128)S(1)} fusion(f32[128,128,512]{2,1,0:T(8,128)} %multiply_reduce_fusion.4, f32[128,512]{1,0:T(8,128)S(1)} %mul.737), kind=kLoop, calls=%fused_computation.22.clone.1 | loop fusion | flops 58703872 | bytes 33882112 | tf_op jit(solution)/shard_map/while/body/eval_jaxpr/reduce_sum | solution.py:32
  102.2 28.7 %multiply_reduce_fusion.4 = f32[128,128,512]{2,1,0:T(8,128)} fusion(f32[128,3,512]{2,1,0:T(4,128)S(1)} %bitcast.105, f32[128,3,128]{2,1,0:T(4,128)S(1)} %get-tuple-element.882), kind=kLoop, calls=%fused_computation.19.clone.1 | loop fusion | flops 67108864 | bytes 34537472 | tf_op jit(solution)/shard_map/while/body/eval_jaxpr/reduce_sum | solution.py:30
  132.0 14.8 %fusion.79 = f32[128,128]{1,0:T(8,128)S(1)} fusion(f32[128,128,512]{2,1,0:T(8,128)} %multiply_reduce_fusion.4, f32[128,512]{1,0:T(8,128)S(1)} %mul.737), kind=kLoop, calls=%fused_computation.22.clone.1 | loop fusion | flops 58703872 | bytes 33882112 | tf_op jit(solution)/shard_map/while/body/eval_jaxpr/reduce_sum | solution.py:32
  149.2 28.7 %multiply_reduce_fusion.4 = f32[128,128,512]{2,1,0:T(8,128)} fusion(f32[128,3,512]{2,1,0:T(4,128)S(1)} %bitcast.105, f32[128,3,128]{2,1,0:T(4,128)S(1)} %get-tuple-element.882), kind=kLoop, calls=%fused_computation.19.clone.1 | loop fusion | flops 67108864 | bytes 34537472 | tf_op jit(solution)/shard_map/while/body/eval_jaxpr/reduce_sum | solution.py:30
  178.9 14.8 %fusion.79 = f32[128,128]{1,0:T(8,128)S(1)} fusion(f32[128,128,512]{2,1,0:T(8,128)} %multiply_reduce_fusion.4, f32[128,512]{1,0:T(8,128)S(1)} %mul.737), kind=kLoop, calls=%fused_computation.22.clone.1 | loop fusion | flops 58703872 | bytes 33882112 | tf_op jit(solution)/shard_map/while/body/eval_jaxpr/reduce_sum | solution.py:32
  196.1 28.7 %multiply_reduce_fusion.4 = f32[128,128,512]{2,1,0:T(8,128)} fusion(f32[128,3,512]{2,1,0:T(4,128)S(1)} %bitcast.105, f32[128,3,128]{2,1,0:T(4,128)S(1)} %get-tuple-element.882), kind=kLoop, calls=%fused_computation.19.clone.1 | loop fusion | flops 67108864 | bytes 34537472 | tf_op jit(solution)/shard_map/while/body/eval_jaxpr/reduce_sum | solution.py:30
  225.8 14.8 %fusion.79 = f32[128,128]{1,0:T(8,128)S(1)} fusion(f32[128,128,512]{2,1,0:T(8,128)} %multiply_reduce_fusion.4, f32[128,512]{1,0:T(8,128)S(1)} %mul.737), kind=kLoop, calls=%fused_computation.22.clone.1 | loop fusion | flops 58703872 | bytes 33882112 | tf_op jit(solution)/shard_map/while/body/eval_jaxpr/reduce_sum | solution.py:32
  271.9 14.7 %fusion.9 = f32[128,3,128]{2,1,0:T(4,128)S(1)} fusion(f32[128,128,128]{2,1,0:T(8,128)S(1)} %multiply_multiply_fusion.6, f32[128,3,128]{2,1,0:T(4,128)S(1)} %get-tuple-element.995), kind=kLoop, calls=%fused_computation.52 | loop fusion | flops 18825216 | bytes 8781824 | tf_op jit(solution)/shard_map/reduce_sum | solution.py:42
  286.7 329.4 %while.54 = (s32[]{:T(128)}, f32[128,3,128]{2,1,0:T(4,128)S(1)}, s32[128,16]{1,0:T(8,128)S(1)}, f32[236,128]{1,0:T(8,128)S(1)}, f32[128,128]{1,0:T(8,128)S(1)}, ...) while((s32[]{:T(128)}, f32[128,3,128]{2,1,0:T(4,128)S(1)}, ...), condition=%wide.region_10.11_spmd, body=%wide.region_7.10_spmd.sunk | while | flops 201378304 | bytes 141250736 | solution.py:87
  289.0 28.8 %fusion.80 = f32[128,128,512]{2,1,0:T(8,128)} fusion(f32[128,3,512]{2,1,0:T(4,128)S(1)} %bitcast.101, f32[128,3,128]{2,1,0:T(4,128)S(1)} %get-tuple-element.918), kind=kLoop, calls=%fused_computation.27.clone.1 | loop fusion | flops 67108864 | bytes 34537472 | tf_op jit(solution)/shard_map/while/body/eval_jaxpr/reduce_sum | solution.py:37
  320.0 24.9 %multiply_multiply_fusion.10 = f32[128,128,512]{2,1,0:T(8,128)} fusion(f32[128,128,512]{2,1,0:T(8,128)} %fusion.80, f32[128,512]{1,0:T(8,128)S(1)} %add.862, f32[128,128]{1,0:T(8,128)S(1)} %get-tuple-element.916, f32[128,512]{1,0:T(8,128)S(1)} %mul.747), kind=kLoop, calls=%fused_computation.29.clone.1 | loop fusion | flops 58720256 | bytes 67698688 | tf_op jit(solution)/shard_map/while/body/eval_jaxpr/mul | solution.py:40
  345.0 23.7 %fusion.81 = f32[128,3,128]{2,1,0:T(4,128)S(1)} fusion(f32[128,128,512]{2,1,0:T(8,128)} %multiply_multiply_fusion.10, f32[128,3,512]{2,1,0:T(4,128)S(1)} %bitcast.102, f32[128,3,128]{2,1,0:T(4,128)S(1)} %get-tuple-element.918), kind=kLoop, calls=%fused_computation.28.clone.1 | loop fusion | flops 75448320 | bytes 34734080 | tf_op jit(solution)/shard_map/while/body/eval_jaxpr/reduce_sum | solution.py:42
  371.4 28.8 %fusion.80 = f32[128,128,512]{2,1,0:T(8,128)} fusion(f32[128,3,512]{2,1,0:T(4,128)S(1)} %bitcast.101, f32[128,3,128]{2,1,0:T(4,128)S(1)} %get-tuple-element.918), kind=kLoop, calls=%fused_computation.27.clone.1 | loop fusion | flops 67108864 | bytes 34537472 | tf_op jit(solution)/shard_map/while/body/eval_jaxpr/reduce_sum | solution.py:37
  402.4 24.9 %multiply_multiply_fusion.10 = f32[128,128,512]{2,1,0:T(8,128)} fusion(f32[128,128,512]{2,1,0:T(8,128)} %fusion.80, f32[128,512]{1,0:T(8,128)S(1)} %add.862, f32[128,128]{1,0:T(8,128)S(1)} %get-tuple-element.916, f32[128,512]{1,0:T(8,128)S(1)} %mul.747), kind=kLoop, calls=%fused_computation.29.clone.1 | loop fusion | flops 58720256 | bytes 67698688 | tf_op jit(solution)/shard_map/while/body/eval_jaxpr/mul | solution.py:40
  427.3 23.7 %fusion.81 = f32[128,3,128]{2,1,0:T(4,128)S(1)} fusion(f32[128,128,512]{2,1,0:T(8,128)} %multiply_multiply_fusion.10, f32[128,3,512]{2,1,0:T(4,128)S(1)} %bitcast.102, f32[128,3,128]{2,1,0:T(4,128)S(1)} %get-tuple-element.918), kind=kLoop, calls=%fused_computation.28.clone.1 | loop fusion | flops 75448320 | bytes 34734080 | tf_op jit(solution)/shard_map/while/body/eval_jaxpr/reduce_sum | solution.py:42
  453.7 28.8 %fusion.80 = f32[128,128,512]{2,1,0:T(8,128)} fusion(f32[128,3,512]{2,1,0:T(4,128)S(1)} %bitcast.101, f32[128,3,128]{2,1,0:T(4,128)S(1)} %get-tuple-element.918), kind=kLoop, calls=%fused_computation.27.clone.1 | loop fusion | flops 67108864 | bytes 34537472 | tf_op jit(solution)/shard_map/while/body/eval_jaxpr/reduce_sum | solution.py:37
  484.7 24.9 %multiply_multiply_fusion.10 = f32[128,128,512]{2,1,0:T(8,128)} fusion(f32[128,128,512]{2,1,0:T(8,128)} %fusion.80, f32[128,512]{1,0:T(8,128)S(1)} %add.862, f32[128,128]{1,0:T(8,128)S(1)} %get-tuple-element.916, f32[128,512]{1,0:T(8,128)S(1)} %mul.747), kind=kLoop, calls=%fused_computation.29.clone.1 | loop fusion | flops 58720256 | bytes 67698688 | tf_op jit(solution)/shard_map/while/body/eval_jaxpr/mul | solution.py:40
  509.7 23.7 %fusion.81 = f32[128,3,128]{2,1,0:T(4,128)S(1)} fusion(f32[128,128,512]{2,1,0:T(8,128)} %multiply_multiply_fusion.10, f32[128,3,512]{2,1,0:T(4,128)S(1)} %bitcast.102, f32[128,3,128]{2,1,0:T(4,128)S(1)} %get-tuple-element.918), kind=kLoop, calls=%fused_computation.28.clone.1 | loop fusion | flops 75448320 | bytes 34734080 | tf_op jit(solution)/shard_map/while/body/eval_jaxpr/reduce_sum | solution.py:42
  536.1 28.8 %fusion.80 = f32[128,128,512]{2,1,0:T(8,128)} fusion(f32[128,3,512]{2,1,0:T(4,128)S(1)} %bitcast.101, f32[128,3,128]{2,1,0:T(4,128)S(1)} %get-tuple-element.918), kind=kLoop, calls=%fused_computation.27.clone.1 | loop fusion | flops 67108864 | bytes 34537472 | tf_op jit(solution)/shard_map/while/body/eval_jaxpr/reduce_sum | solution.py:37
  567.1 24.9 %multiply_multiply_fusion.10 = f32[128,128,512]{2,1,0:T(8,128)} fusion(f32[128,128,512]{2,1,0:T(8,128)} %fusion.80, f32[128,512]{1,0:T(8,128)S(1)} %add.862, f32[128,128]{1,0:T(8,128)S(1)} %get-tuple-element.916, f32[128,512]{1,0:T(8,128)S(1)} %mul.747), kind=kLoop, calls=%fused_computation.29.clone.1 | loop fusion | flops 58720256 | bytes 67698688 | tf_op jit(solution)/shard_map/while/body/eval_jaxpr/mul | solution.py:40
  592.0 23.7 %fusion.81 = f32[128,3,128]{2,1,0:T(4,128)S(1)} fusion(f32[128,128,512]{2,1,0:T(8,128)} %multiply_multiply_fusion.10, f32[128,3,512]{2,1,0:T(4,128)S(1)} %bitcast.102, f32[128,3,128]{2,1,0:T(4,128)S(1)} %get-tuple-element.918), kind=kLoop, calls=%fused_computation.28.clone.1 | loop fusion | flops 75448320 | bytes 34734080 | tf_op jit(solution)/shard_map/while/body/eval_jaxpr/reduce_sum | solution.py:42
  663.2 11.5 fusion.10
  682.7 187.7 %while.55 = (s32[]{:T(128)}, f32[128,128]{1,0:T(8,128)S(1)}, s32[128,16]{1,0:T(8,128)S(1)}, f32[236,128]{1,0:T(8,128)S(1)}, f32[128,3,128]{2,1,0:T(4,128)S(1)}, ...) while((s32[]{:T(128)}, f32[128,128]{1,0:T(8,128)S(1)}, ...), condition=%wide.region_21.22_spmd, body=%wide.region_18.21_spmd.sunk | while | flops 125831688 | bytes 71256216 | solution.py:71
  685.1 28.7 %multiply_reduce_fusion.5 = f32[128,128,512]{2,1,0:T(8,128)} fusion(f32[128,3,512]{2,1,0:T(4,128)S(1)} %bitcast.106, f32[128,3,128]{2,1,0:T(4,128)S(1)} %get-tuple-element.948), kind=kLoop, calls=%fused_computation.33.clone.1 | loop fusion | flops 67108864 | bytes 34537472 | tf_op jit(solution)/shard_map/while/body/eval_jaxpr/reduce_sum | solution.py:30
  714.8 14.8 %fusion.82 = f32[128,128]{1,0:T(8,128)S(1)} fusion(f32[128,128,512]{2,1,0:T(8,128)} %multiply_reduce_fusion.5, f32[128,512]{1,0:T(8,128)S(1)} %mul.754), kind=kLoop, calls=%fused_computation.36.clone.1 | loop fusion | flops 58703872 | bytes 33882112 | tf_op jit(solution)/shard_map/while/body/eval_jaxpr/reduce_sum | solution.py:32
  732.0 28.7 %multiply_reduce_fusion.5 = f32[128,128,512]{2,1,0:T(8,128)} fusion(f32[128,3,512]{2,1,0:T(4,128)S(1)} %bitcast.106, f32[128,3,128]{2,1,0:T(4,128)S(1)} %get-tuple-element.948), kind=kLoop, calls=%fused_computation.33.clone.1 | loop fusion | flops 67108864 | bytes 34537472 | tf_op jit(solution)/shard_map/while/body/eval_jaxpr/reduce_sum | solution.py:30
  761.7 14.8 %fusion.82 = f32[128,128]{1,0:T(8,128)S(1)} fusion(f32[128,128,512]{2,1,0:T(8,128)} %multiply_reduce_fusion.5, f32[128,512]{1,0:T(8,128)S(1)} %mul.754), kind=kLoop, calls=%fused_computation.36.clone.1 | loop fusion | flops 58703872 | bytes 33882112 | tf_op jit(solution)/shard_map/while/body/eval_jaxpr/reduce_sum | solution.py:32
  778.9 28.7 %multiply_reduce_fusion.5 = f32[128,128,512]{2,1,0:T(8,128)} fusion(f32[128,3,512]{2,1,0:T(4,128)S(1)} %bitcast.106, f32[128,3,128]{2,1,0:T(4,128)S(1)} %get-tuple-element.948), kind=kLoop, calls=%fused_computation.33.clone.1 | loop fusion | flops 67108864 | bytes 34537472 | tf_op jit(solution)/shard_map/while/body/eval_jaxpr/reduce_sum | solution.py:30
  808.7 14.8 %fusion.82 = f32[128,128]{1,0:T(8,128)S(1)} fusion(f32[128,128,512]{2,1,0:T(8,128)} %multiply_reduce_fusion.5, f32[128,512]{1,0:T(8,128)S(1)} %mul.754), kind=kLoop, calls=%fused_computation.36.clone.1 | loop fusion | flops 58703872 | bytes 33882112 | tf_op jit(solution)/shard_map/while/body/eval_jaxpr/reduce_sum | solution.py:32
  825.8 28.7 %multiply_reduce_fusion.5 = f32[128,128,512]{2,1,0:T(8,128)} fusion(f32[128,3,512]{2,1,0:T(4,128)S(1)} %bitcast.106, f32[128,3,128]{2,1,0:T(4,128)S(1)} %get-tuple-element.948), kind=kLoop, calls=%fused_computation.33.clone.1 | loop fusion | flops 67108864 | bytes 34537472 | tf_op jit(solution)/shard_map/while/body/eval_jaxpr/reduce_sum | solution.py:30
  855.6 14.8 %fusion.82 = f32[128,128]{1,0:T(8,128)S(1)} fusion(f32[128,128,512]{2,1,0:T(8,128)} %multiply_reduce_fusion.5, f32[128,512]{1,0:T(8,128)S(1)} %mul.754), kind=kLoop, calls=%fused_computation.36.clone.1 | loop fusion | flops 58703872 | bytes 33882112 | tf_op jit(solution)/shard_map/while/body/eval_jaxpr/reduce_sum | solution.py:32
  901.4 14.7 %fusion.11 = f32[128,3,128]{2,1,0:T(4,128)S(1)} fusion(f32[128,128,128]{2,1,0:T(8,128)S(1)} %multiply_multiply_fusion.4, f32[128,3,128]{2,1,0:T(4,128)S(1)} %get-tuple-element.994), kind=kLoop, calls=%fused_computation.54 | loop fusion | flops 18825216 | bytes 8781824 | tf_op jit(solution)/shard_map/reduce_sum | solution.py:42
  916.2 329.4 %while.56 = (s32[]{:T(128)}, f32[128,3,128]{2,1,0:T(4,128)S(1)}, s32[128,16]{1,0:T(8,128)S(1)}, f32[236,128]{1,0:T(8,128)S(1)}, f32[128,128]{1,0:T(8,128)S(1)}, ...) while((s32[]{:T(128)}, f32[128,3,128]{2,1,0:T(4,128)S(1)}, ...), condition=%wide.region_26.27_spmd, body=%wide.region_23.26_spmd.sunk | while | flops 201378304 | bytes 141250736 | solution.py:87
  918.5 28.8 %fusion.83 = f32[128,128,512]{2,1,0:T(8,128)} fusion(f32[128,3,512]{2,1,0:T(4,128)S(1)} %bitcast.103, f32[128,3,128]{2,1,0:T(4,128)S(1)} %get-tuple-element.984), kind=kLoop, calls=%fused_computation.41.clone.1 | loop fusion | flops 67108864 | bytes 34537472 | tf_op jit(solution)/shard_map/while/body/eval_jaxpr/reduce_sum | solution.py:37
  949.6 24.9 %multiply_multiply_fusion.11 = f32[128,128,512]{2,1,0:T(8,128)} fusion(f32[128,128,512]{2,1,0:T(8,128)} %fusion.83, f32[128,512]{1,0:T(8,128)S(1)} %add.874, f32[128,128]{1,0:T(8,128)S(1)} %get-tuple-element.982, f32[128,512]{1,0:T(8,128)S(1)} %mul.764), kind=kLoop, calls=%fused_computation.43.clone.1 | loop fusion | flops 58720256 | bytes 67698688 | tf_op jit(solution)/shard_map/while/body/eval_jaxpr/mul | solution.py:40
  974.5 23.7 %fusion.84 = f32[128,3,128]{2,1,0:T(4,128)S(1)} fusion(f32[128,128,512]{2,1,0:T(8,128)} %multiply_multiply_fusion.11, f32[128,3,512]{2,1,0:T(4,128)S(1)} %bitcast.104, f32[128,3,128]{2,1,0:T(4,128)S(1)} %get-tuple-element.984), kind=kLoop, calls=%fused_computation.42.clone.1 | loop fusion | flops 75448320 | bytes 34734080 | tf_op jit(solution)/shard_map/while/body/eval_jaxpr/reduce_sum | solution.py:42
  1000.9 28.8 %fusion.83 = f32[128,128,512]{2,1,0:T(8,128)} fusion(f32[128,3,512]{2,1,0:T(4,128)S(1)} %bitcast.103, f32[128,3,128]{2,1,0:T(4,128)S(1)} %get-tuple-element.984), kind=kLoop, calls=%fused_computation.41.clone.1 | loop fusion | flops 67108864 | bytes 34537472 | tf_op jit(solution)/shard_map/while/body/eval_jaxpr/reduce_sum | solution.py:37
  1031.9 24.9 %multiply_multiply_fusion.11 = f32[128,128,512]{2,1,0:T(8,128)} fusion(f32[128,128,512]{2,1,0:T(8,128)} %fusion.83, f32[128,512]{1,0:T(8,128)S(1)} %add.874, f32[128,128]{1,0:T(8,128)S(1)} %get-tuple-element.982, f32[128,512]{1,0:T(8,128)S(1)} %mul.764), kind=kLoop, calls=%fused_computation.43.clone.1 | loop fusion | flops 58720256 | bytes 67698688 | tf_op jit(solution)/shard_map/while/body/eval_jaxpr/mul | solution.py:40
  1056.8 23.7 %fusion.84 = f32[128,3,128]{2,1,0:T(4,128)S(1)} fusion(f32[128,128,512]{2,1,0:T(8,128)} %multiply_multiply_fusion.11, f32[128,3,512]{2,1,0:T(4,128)S(1)} %bitcast.104, f32[128,3,128]{2,1,0:T(4,128)S(1)} %get-tuple-element.984), kind=kLoop, calls=%fused_computation.42.clone.1 | loop fusion | flops 75448320 | bytes 34734080 | tf_op jit(solution)/shard_map/while/body/eval_jaxpr/reduce_sum | solution.py:42
  1083.2 28.8 %fusion.83 = f32[128,128,512]{2,1,0:T(8,128)} fusion(f32[128,3,512]{2,1,0:T(4,128)S(1)} %bitcast.103, f32[128,3,128]{2,1,0:T(4,128)S(1)} %get-tuple-element.984), kind=kLoop, calls=%fused_computation.41.clone.1 | loop fusion | flops 67108864 | bytes 34537472 | tf_op jit(solution)/shard_map/while/body/eval_jaxpr/reduce_sum | solution.py:37
  1114.3 24.9 %multiply_multiply_fusion.11 = f32[128,128,512]{2,1,0:T(8,128)} fusion(f32[128,128,512]{2,1,0:T(8,128)} %fusion.83, f32[128,512]{1,0:T(8,128)S(1)} %add.874, f32[128,128]{1,0:T(8,128)S(1)} %get-tuple-element.982, f32[128,512]{1,0:T(8,128)S(1)} %mul.764), kind=kLoop, calls=%fused_computation.43.clone.1 | loop fusion | flops 58720256 | bytes 67698688 | tf_op jit(solution)/shard_map/while/body/eval_jaxpr/mul | solution.py:40
  1139.2 23.7 %fusion.84 = f32[128,3,128]{2,1,0:T(4,128)S(1)} fusion(f32[128,128,512]{2,1,0:T(8,128)} %multiply_multiply_fusion.11, f32[128,3,512]{2,1,0:T(4,128)S(1)} %bitcast.104, f32[128,3,128]{2,1,0:T(4,128)S(1)} %get-tuple-element.984), kind=kLoop, calls=%fused_computation.42.clone.1 | loop fusion | flops 75448320 | bytes 34734080 | tf_op jit(solution)/shard_map/while/body/eval_jaxpr/reduce_sum | solution.py:42
  1165.6 28.8 %fusion.83 = f32[128,128,512]{2,1,0:T(8,128)} fusion(f32[128,3,512]{2,1,0:T(4,128)S(1)} %bitcast.103, f32[128,3,128]{2,1,0:T(4,128)S(1)} %get-tuple-element.984), kind=kLoop, calls=%fused_computation.41.clone.1 | loop fusion | flops 67108864 | bytes 34537472 | tf_op jit(solution)/shard_map/while/body/eval_jaxpr/reduce_sum | solution.py:37
  1196.6 24.9 %multiply_multiply_fusion.11 = f32[128,128,512]{2,1,0:T(8,128)} fusion(f32[128,128,512]{2,1,0:T(8,128)} %fusion.83, f32[128,512]{1,0:T(8,128)S(1)} %add.874, f32[128,128]{1,0:T(8,128)S(1)} %get-tuple-element.982, f32[128,512]{1,0:T(8,128)S(1)} %mul.764), kind=kLoop, calls=%fused_computation.43.clone.1 | loop fusion | flops 58720256 | bytes 67698688 | tf_op jit(solution)/shard_map/while/body/eval_jaxpr/mul | solution.py:40
  1221.5 23.7 %fusion.84 = f32[128,3,128]{2,1,0:T(4,128)S(1)} fusion(f32[128,128,512]{2,1,0:T(8,128)} %multiply_multiply_fusion.11, f32[128,3,512]{2,1,0:T(4,128)S(1)} %bitcast.104, f32[128,3,128]{2,1,0:T(4,128)S(1)} %get-tuple-element.984), kind=kLoop, calls=%fused_computation.42.clone.1 | loop fusion | flops 75448320 | bytes 34734080 | tf_op jit(solution)/shard_map/while/body/eval_jaxpr/reduce_sum | solution.py:42
  (320 shorter events, 225.1 us)
Async XLA Ops:
  9.5 26.0 %collective-permute-start = (f32[1,3,3,4,4,128]{5,4,3,2,1,0:T(4,128)S(1)}, f32[1,3,3,4,4,128]{5,4,3,2,1,0:T(4,128)S(1)}, u32[]{:S(2)}, u32[]{:S(2)}) collective-permute-start(f32[1,3,3,4,4,128]{5,4,3,2,1,0:T(4,128)S(1)} %bitcast.124), channel_id=1, source_target_pairs={{0,8},{8,16},{16,24},{1,9},{9,17},{17,25},{2,10},{10,18},{18,26},{... | collective-permute-start | bytes 221192 | tf_op jit(solution)/shard_map/ppermute | solution.py:20
  14.4 21.1 %collective-permute-start.1 = (f32[1,3,3,4,4,128]{5,4,3,2,1,0:T(4,128)S(1)}, f32[1,3,3,4,4,128]{5,4,3,2,1,0:T(4,128)S(1)}, u32[]{:S(2)}, u32[]{:S(2)}) collective-permute-start(f32[1,3,3,4,4,128]{5,4,3,2,1,0:T(4,128)S(1)} %bitcast.123), channel_id=1, source_target_pairs={{8,0},{16,8},{24,16},{9,1},{17,9},{25,17},{10,2},{18,10},{26,18},{... | collective-permute-start | bytes 221192 | tf_op jit(solution)/shard_map/ppermute | solution.py:23
  35.6 5.9 collective-permute-start.2
  39.1 6.8 collective-permute-start.3
  46.0 2.9 collective-permute-start.4
  47.3 3.3 collective-permute-start.5
  53.0 213.4 %copy-start.3 = (f32[128,128]{1,0:T(8,128)S(1)}, f32[128,128]{1,0:T(8,128)}, u32[]{:S(2)}) copy-start(f32[128,128]{1,0:T(8,128)} %param.32) | copy-start | bytes 196612
  241.5 6.0 collective-permute-start.6
  246.1 6.0 collective-permute-start.7
  252.1 5.0 collective-permute-start.8
  255.6 5.8 collective-permute-start.9
  261.4 4.8 collective-permute-start.10
  262.7 3.5 collective-permute-start.11
  286.7 329.5 %copy-start.5 = (f32[128,3,128]{2,0,1:T(8,128)S(1)}, f32[128,3,128]{2,0,1:T(8,128)}, u32[]{:S(2)}) copy-start(f32[128,3,128]{2,0,1:T(8,128)} %param.30) | copy-start | bytes 589828
  286.7 330.7 %copy-start.4 = (f32[128,128]{1,0:T(8,128)S(1)}, f32[128,128]{1,0:T(8,128)}, u32[]{:S(2)}) copy-start(f32[128,128]{1,0:T(8,128)} %param.32) | copy-start | bytes 196612
  286.7 330.7 %copy-start.7 = (f32[128,1,1]{2,1,0:T(1,128)S(1)}, f32[128,1,1]{2,1,0:T(1,128)}, u32[]{:S(2)}) copy-start(f32[128,1,1]{2,1,0:T(1,128)} %copy.131) | copy-start | bytes 1540
  286.7 358.5 %copy-start.6 = (s32[1024]{0:T(1024)S(1)}, s32[1024]{0:T(1024)}, u32[]{:S(2)}) copy-start(s32[1024]{0:T(1024)} %get-tuple-element.684) | copy-start | bytes 12292
  616.1 66.6 %copy-start.1 = (s32[128,16]{1,0:T(8,128)S(1)}, s32[128,16]{1,0:T(8,128)}, u32[]{:S(2)}) copy-start(s32[128,16]{1,0:T(8,128)} %copy.137) | copy-start | bytes 24580
  622.5 18.1 %collective-permute-start.12 = (f32[1,2,8,128]{3,2,1,0:T(8,128)S(1)}, f32[1,2,8,128]{3,2,1,0:T(8,128)S(1)}, u32[]{:S(2)}, u32[]{:S(2)}) collective-permute-start(f32[1,2,8,128]{3,2,1,0:T(8,128)S(1)} %get-tuple-element.675), channel_id=1, source_target_pairs={{0,8},{8,16},{16,24},{1,9},{9,17},{17,25},{2,10},{10,18},{18,26},{... | collective-permute-start | bytes 24584 | tf_op jit(solution)/shard_map/ppermute | solution.py:20
  627.5 14.4 %collective-permute-start.13 = (f32[1,2,8,128]{3,2,1,0:T(8,128)S(1)}, f32[1,2,8,128]{3,2,1,0:T(8,128)S(1)}, u32[]{:S(2)}, u32[]{:S(2)}) collective-permute-start(f32[1,2,8,128]{3,2,1,0:T(8,128)S(1)} %get-tuple-element.674), channel_id=1, source_target_pairs={{8,0},{16,8},{24,16},{9,1},{17,9},{25,17},{10,2},{18,10},{26,18},{... | collective-permute-start | bytes 24584 | tf_op jit(solution)/shard_map/ppermute | solution.py:23
  628.8 13.1 %collective-permute-start.14 = (f32[1,2,8,128]{3,2,1,0:T(8,128)S(1)}, f32[1,2,8,128]{3,2,1,0:T(8,128)S(1)}, u32[]{:S(2)}, u32[]{:S(2)}) collective-permute-start(f32[1,2,8,128]{3,2,1,0:T(8,128)S(1)} %get-tuple-element.673), channel_id=1, source_target_pairs={{0,2},{2,4},{4,6},{1,3},{3,5},{5,7},{8,10},{10,12},{12,14},{9,11},... | collective-permute-start | bytes 24584 | tf_op jit(solution)/shard_map/ppermute | solution.py:20
  632.3 9.6 collective-permute-start.15
  633.6 8.4 collective-permute-start.16
  640.5 3.1 collective-permute-start.17
  644.9 32.4 %copy-start.2 = (f32[128,7,128]{2,1,0:T(8,128)}, f32[128,7,128]{2,1,0:T(8,128)S(1)}, u32[]{:S(2)}) copy-start(f32[128,7,128]{2,1,0:T(8,128)S(1)} %scatter_fusion.2) | copy-start | bytes 1376260
  646.8 6.5 collective-permute-start.18
  651.1 6.2 collective-permute-start.19
  657.4 17.3 %collective-permute-start.20 = (f32[5,1,3,4,4,128]{5,4,3,2,1,0:T(4,128)S(1)}, f32[5,1,3,4,4,128]{5,4,3,2,1,0:T(4,128)S(1)}, u32[]{:S(2)}, u32[]{:S(2)}) collective-permute-start(f32[5,1,3,4,4,128]{5,4,3,2,1,0:T(4,128)S(1)} %get-tuple-element.650), channel_id=1, source_target_pairs={{0,2},{2,4},{4,6},{1,3},{3,5},{5,7},{8,10},{10,12},{12,14},{9,11},... | collective-permute-start | bytes 368648 | tf_op jit(solution)/shard_map/ppermute | solution.py:20
  661.7 13.0 %collective-permute-start.21 = (f32[5,1,3,4,4,128]{5,4,3,2,1,0:T(4,128)S(1)}, f32[5,1,3,4,4,128]{5,4,3,2,1,0:T(4,128)S(1)}, u32[]{:S(2)}, u32[]{:S(2)}) collective-permute-start(f32[5,1,3,4,4,128]{5,4,3,2,1,0:T(4,128)S(1)} %get-tuple-element.651), channel_id=1, source_target_pairs={{2,0},{4,2},{6,4},{3,1},{5,3},{7,5},{10,8},{12,10},{14,12},{11,9},... | collective-permute-start | bytes 368648 | tf_op jit(solution)/shard_map/ppermute | solution.py:23
  674.7 7.3 collective-permute-start.22
  676.0 6.0 collective-permute-start.23
  682.7 188.4 %copy-start.9 = (pred[27,4]{1,0:T(8,128)(4,1)S(1)}, pred[27,4]{1,0:T(8,128)(4,1)}, u32[]{:S(2)}) copy-start(pred[27,4]{1,0:T(8,128)(4,1)} %get-tuple-element.678) | copy-start | bytes 328
  682.7 193.8 %copy-start.8 = (pred[3,3,3,4]{3,2,1,0:T(4,128)(4,1)S(1)}, pred[3,3,3,4]{3,2,1,0:T(4,128)(4,1)}, u32[]{:S(2)}) copy-start(pred[3,3,3,4]{3,2,1,0:T(4,128)(4,1)} %get-tuple-element.676) | copy-start | bytes 328
  870.4 45.8 %copy-start = (f32[128,128]{1,0:T(8,128)}, f32[128,128]{1,0:T(8,128)S(1)}, u32[]{:S(2)}) copy-start(f32[128,128]{1,0:T(8,128)S(1)} %get-tuple-element.579) | copy-start | bytes 196612
  871.3 5.5 collective-permute-start.24
  875.3 5.7 collective-permute-start.25
  881.0 6.1 collective-permute-start.26
  885.6 5.8 collective-permute-start.27
  891.4 2.9 collective-permute-start.28
  892.7 3.1 collective-permute-start.29
where the time goes:
time: 1260 us; the launch traced here: 1250 us
  other arithmetic  1060 us (84%)
  local copies, waits for them, and re-layouts  81.7 us (6%)
  starting transfers between devices  69.4 us (6%)
  waiting for transfers between devices  31.8 us (3%)
    reduce_sum x10, other arithmetic, pair_density(): squared = jnp.sum(offset * offset, axis=1)  252 us
    reduce_sum x8, other arithmetic, pair_force(): squared = jnp.sum(offset * offset, axis=1)  231 us
    reduce_sum x10, other arithmetic, pair_force(): jnp.sum(weight[:, None, :, :] * offset, axis=3)  219 us
    mul x10, other arithmetic, pair_force(): away_mass[:, None, :] * (home_term[:, :, None] + away_term[:, None, :])  210 us
    reduce_sum x10, other arithmetic, pair_density(): return jnp.sum(away_mass[:, None, :] * (kernel * kernel * kernel), axis=2)  128 us
    ppermute x15, starting transfers between devices, padded_2(): lax.ppermute(lax.slice_in_dim(block, block.shape[dim] - width, None, axis...  49.4 us
    gather x16, local copies, waits for them, and re-layouts, joined_points(): chosen = all_points[picked]  33.2 us
    ppermute x15, waiting for transfers between devices, padded_2(): lax.ppermute(lax.slice_in_dim(block, 0, width, axis=dim), axis, backward)  30.8 us
  transfers between devices with their start and end apart: 30, of which 12 were waited for; matrix products, arithmetic and copies ran while one was open for 4% of the time, Pallas kernels for 0%

commit v1 on v0

--- a/solution.py
+++ b/solution.py
@@ -2,6 +2,8 @@
 import jax.numpy as jnp
 import numpy as np
 from jax import lax
+from jax.experimental import pallas as pl
+from jax.experimental.pallas import tpu as pltpu
 from jax.sharding import PartitionSpec as P
 
 MOVE_CAP = 2
@@ -9,7 +11,6 @@
 
 smooth_len = 0.5
 time_step = 0.25
-column_group = 4
 
 
 def padded_2(block, sides, width):
@@ -25,66 +26,147 @@
     return block
 
 
-def pair_density(home_points, away_points, away_mass):
-    offset = home_points[:, :, :, None] - away_points[:, :, None, :]
-    squared = jnp.sum(offset * offset, axis=1)
-    kernel = jnp.maximum(1.0 - squared / (smooth_len * smooth_len), 0.0)
-    return jnp.sum(away_mass[:, None, :] * (kernel * kernel * kernel), axis=2)
-
-
-def pair_force(home_points, home_term, away_points, away_mass, away_term):
-    offset = home_points[:, :, :, None] - away_points[:, :, None, :]
-    squared = jnp.sum(offset * offset, axis=1)
-    kernel = jnp.maximum(1.0 - squared / (smooth_len * smooth_len), 0.0)
-    weight = (
-        away_mass[:, None, :] * (home_term[:, :, None] + away_term[:, None, :]) * kernel * kernel
-    )
-    return 6.0 / (smooth_len * smooth_len) * jnp.sum(weight[:, None, :, :] * offset, axis=3)
-
-
 def pressure_term(density):
     return jnp.exp(jnp.log(density) * (-1.0 / 3.0))
 
 
-def joined_points(all_points, picked):
-    chosen = all_points[picked]
-    rows = chosen.shape[0]
-    return jnp.transpose(chosen, (0, 2, 1, 3)).reshape(
-        rows, chosen.shape[2], chosen.shape[1] * chosen.shape[3]
-    )
-
-
-def joined_values(all_values, picked):
-    chosen = all_values[picked]
-    return chosen.reshape(chosen.shape[0], chosen.shape[1] * chosen.shape[2])
-
-
-def table_density(home_points, home_mass, all_points, all_mass, lookup):
-    initial = pair_density(home_points, home_points, home_mass)
-
-    def add_group(group, running):
-        picked = lax.dynamic_slice_in_dim(lookup, group * column_group, column_group, 1)
-        return running + pair_density(
-            home_points, joined_points(all_points, picked), joined_values(all_mass, picked)
+PART_PAIRS = ((0, 0), (0, 1), (1, 0), (0, 2), (2, 0), (1, 1))
+INVERSE = 1.0 / (smooth_len * smooth_len)
+
+
+def three_parts(value):
+    parts = []
+    for _ in range(3):
+        part = value.astype(jnp.bfloat16).astype(jnp.float32)
+        parts.append(part)
+        value = value - part
+    return parts
+
+
+def cube_root(mass):
+    return jnp.exp(jnp.log(mass) * (1.0 / 3.0))
+
+
+def density_kernel(lookup, stacked, out, home, away):
+    blocks, columns = lookup.shape
+
+    def prepare(r, carry):
+        tile = stacked[r]
+        here = tile[0:3]
+        root = cube_root(tile[3:4])
+        square = jnp.sum(here * here, axis=0, keepdims=True)
+        one = jnp.ones_like(square)
+        blank = jnp.zeros_like(here)
+        far = jnp.concatenate(
+            [2.0 * INVERSE * root * here, -INVERSE * root * square, root, blank], axis=0
         )
-
-    return lax.fori_loop(0, lookup.shape[1] // column_group, add_group, initial)
-
-
-def table_force(home_points, home_mass, home_term, all_points, all_mass, all_term, lookup):
-    initial = pair_force(home_points, home_term, home_points, home_mass, home_term)
-
-    def add_group(group, running):
-        picked = lax.dynamic_slice_in_dim(lookup, group * column_group, column_group, 1)
-        return running + pair_force(
-            home_points,
-            home_term,
-            joined_points(all_points, picked),
-            joined_values(all_mass, picked),
-            joined_values(all_term, picked),
+        near = jnp.concatenate([here, one, 1.0 - INVERSE * square, blank], axis=0)
+        far_parts = three_parts(far)
+        near_parts = three_parts(near)
+        rows = jnp.concatenate([far_parts[a] for a, _ in PART_PAIRS], axis=0)
+        away[r] = rows.T.astype(jnp.bfloat16)
+        home[r] = jnp.concatenate([near_parts[b] for _, b in PART_PAIRS], axis=0).astype(
+            jnp.bfloat16
         )
-
-    return lax.fori_loop(0, lookup.shape[1] // column_group, add_group, initial)
+        return carry
+
+    lax.fori_loop(0, stacked.shape[0], prepare, 0, unroll=4)
+
+    def one_block(b, carry):
+        rhs = home[b]
+        acc = jnp.zeros((8, rhs.shape[1]), jnp.float32)
+        for k in range(columns + 1):
+            row = b if k == 0 else lookup[b, k - 1]
+            w = jnp.dot(away[row], rhs, preferred_element_type=jnp.float32)
+            w = jnp.maximum(w, 0.0)
+            w = w * w * w
+            acc = acc + jnp.sum(w.reshape(w.shape[0] // 8, 8, w.shape[1]), axis=0)
+        out[pl.ds(b, 1), :] = jnp.sum(acc, axis=0, keepdims=True)
+        return carry
+
+    lax.fori_loop(0, blocks, one_block, 0)
+
+
+def force_kernel(lookup, home, away, stacked, term, out, moment):
+    blocks, columns = lookup.shape
+
+    def prepare(r, carry):
+        tile = stacked[r]
+        root = cube_root(tile[3:4])
+        q = term[pl.ds(r, 1), :]
+        plain = jnp.concatenate([root, root * tile[0:3]], axis=0)
+        full = jnp.concatenate([plain, plain * q], axis=0)
+        high = full.astype(jnp.bfloat16).astype(jnp.float32)
+        moment[r] = jnp.concatenate([high, full - high], axis=0).astype(jnp.bfloat16)
+        return carry
+
+    lax.fori_loop(0, stacked.shape[0], prepare, 0, unroll=4)
+
+    def one_block(b, carry):
+        rhs = home[b]
+        acc = jnp.zeros((16, 2 * rhs.shape[1]), jnp.float32)
+        rows = [b] + [lookup[b, k] for k in range(columns)]
+        for start in range(0, columns + 1, GROUP):
+            group = rows[start : start + GROUP]
+            parts = []
+            for row in group:
+                w = jnp.dot(away[row], rhs, preferred_element_type=jnp.float32)
+                w = jnp.maximum(w, 0.0)
+                w = w * w
+                high = w.astype(jnp.bfloat16)
+                low = (w - high.astype(jnp.float32)).astype(jnp.bfloat16)
+                parts.append(jnp.concatenate([high, low], axis=1))
+            feature = jnp.concatenate([moment[row] for row in group], axis=1)
+            both = jnp.concatenate(parts, axis=0)
+            acc = acc + jnp.dot(feature, both, preferred_element_type=jnp.float32)
+        acc = acc[:, : rhs.shape[1]] + acc[:, rhs.shape[1] :]
+        sums = acc[0:8] + acc[8:16]
+        q = term[pl.ds(b, 1), :]
+        here = stacked[b][0:3]
+        near = here * sums[0:1] - sums[1:4]
+        far = here * sums[4:5] - sums[5:8]
+        out[b] = 6.0 * INVERSE * (q * near + far)
+        return carry
+
+    lax.fori_loop(0, blocks, one_block, 0)
+
+
+GROUP = 2
+
+
+def kernel_call(body, out_shape, operands, scratch=()):
+    vmem = pl.BlockSpec(memory_space=pltpu.VMEM)
+    smem = pl.BlockSpec(memory_space=pltpu.SMEM)
+    return pl.pallas_call(
+        body,
+        out_shape=out_shape,
+        in_specs=[smem] + [vmem] * (len(operands) - 1),
+        out_specs=jax.tree.map(lambda _: vmem, out_shape),
+        scratch_shapes=scratch,
+    )(*operands)
+
+
+def pair_sums(stacked, lookup, finish_term):
+    blocks = lookup.shape[0]
+    total, _, width = stacked.shape
+    depth = 8 * len(PART_PAIRS)
+    density, home, away = kernel_call(
+        density_kernel,
+        (
+            jax.ShapeDtypeStruct((blocks, width), jnp.float32),
+            jax.ShapeDtypeStruct((total, depth, width), jnp.bfloat16),
+            jax.ShapeDtypeStruct((total, width, depth), jnp.bfloat16),
+        ),
+        (lookup, stacked),
+    )
+    all_term = finish_term(density)
+    acceleration = kernel_call(
+        force_kernel,
+        jax.ShapeDtypeStruct((blocks, 3, width), jnp.float32),
+        (lookup, home, away, stacked, all_term),
+        [pltpu.VMEM((total, 16, width), jnp.bfloat16)],
+    )
+    return (density, acceleration)
 
 
 def near_slots(sender_rows):
@@ -148,15 +230,15 @@
     payload = jnp.concatenate([points, weights[:, None, :]], axis=1)
     stacked = jnp.concatenate([payload, ghost_blocks(payload, sender_rows)], axis=0)
     lookup = table_rows(neighbours, blocks, sender_rows.shape[1])
-    all_points = stacked[:, 0:3]
-    all_mass = stacked[:, 3]
-    density = table_density(points, weights, all_points, all_mass, lookup)
-    all_rho = jnp.concatenate([density, ghost_density(density, sender_rows)], axis=0)
-    all_term = pressure_term(all_rho)
-    acceleration = table_force(
-        points, weights, all_term[:blocks], all_points, all_mass, all_term, lookup
-    )
-    return (density, acceleration)
+    middle = [lax.axis_index(axis).astype(jnp.float32) + 0.5 for axis in ("gx", "gy", "gz")]
+    middle = jnp.stack(middle + [jnp.float32(0.0)])
+    stacked = stacked - middle[None, :, None]
+
+    def finish_term(density):
+        all_rho = jnp.concatenate([density, ghost_density(density, sender_rows)], axis=0)
+        return pressure_term(all_rho)
+
+    return pair_sums(stacked, lookup, finish_term)
 
 
 def migrate(fields, destination):

time: 1260 us -> 434 us (0.34)
  other arithmetic: 1060 us -> 18.7 us
  Pallas kernels: 0 us -> 285 us
  local copies, waits for them, and re-layouts: 81.7 us -> 23.1 us
    reduce_sum x38 -> x0, other arithmetic: 830 us -> none  [the longest x10 252 us: pair_density(): squared = jnp.sum(offset * offset, axis=1)]
    pallas_call x0 -> x4, Pallas kernels: none -> 285 us  [kernel_call(): pl.pallas_call(body, out_shape=out_shape, in_specs=[smem] + [vmem] * (len...]
    mul x12 -> x0, other arithmetic: 210 us -> none  [the longest x10 210 us: pair_force(): away_mass[:, None, :] * (home_term[:, :, None] + away_term[:, None, :])]
    gather x40 -> x0, local copies, waits for them, and re-layouts: 58 us -> none  [the longest x16 33.2 us: joined_points(): chosen = all_points[picked]]
  transfers between devices with their start and end apart: 30 -> 30, of which waited for: 12 -> 17; matrix products, arithmetic and copies ran while one was open for 4% -> 3% of each run, Pallas kernels for 0% -> 0%
where the time goes in v1:
time: 434 us; the launch traced here: 433 us
  Pallas kernels  285 us (66%)
  starting transfers between devices  65.2 us (15%)
  waiting for transfers between devices  38.9 us (9%)
  local copies, waits for them, and re-layouts  23.1 us (5%)
  other arithmetic  18.7 us (4%)
    pallas_call x4, Pallas kernels, kernel_call(): pl.pallas_call(body, out_shape=out_shape, in_specs=[smem] + [vmem] * (len...  285 us
    ppermute x15, starting transfers between devices, padded_2(): lax.ppermute(lax.slice_in_dim(block, block.shape[dim] - width, None, axis...  45.9 us
    ppermute x15, waiting for transfers between devices, padded_2(): lax.ppermute(lax.slice_in_dim(block, 0, width, axis=dim), axis, backward)  36.9 us
    ppermute x15, starting transfers between devices, padded_2(): lax.ppermute(lax.slice_in_dim(block, 0, width, axis=dim), axis, backward)  19.4 us
  transfers between devices with their start and end apart: 30, of which 17 were waited for; matrix products, arithmetic and copies ran while one was open for 3% of the time, Pallas kernels for 0%

profile of v1, /device:TPU:0, one launch (start us, length us, event | category | flops | bytes accessed | tf_op | source)
XLA Modules:
  0.0 432.6 jit_solution(3283227257777826812)
XLA Ops:
  8.4 4.9 %collective-permute-start = (f32[1,3,3,4,4,128]{5,4,3,2,1,0:T(4,128)S(1)}, f32[1,3,3,4,4,128]{5,4,3,2,1,0:T(4,128)S(1)}, u32[]{:S(2)}, u32[]{:S(2)}) collective-permute-start(f32[1,3,3,4,4,128]{5,4,3,2,1,0:T(4,128)S(1)} %bitcast.79), channel_id=1, source_target_pairs={{0,8},{8,16},{16,24},{1,9},{9,17},{17,25},{2,10},{10,18},{18,26},{... | collective-permute-start | bytes 221192 | tf_op jit(solution)/shard_map/ppermute | solution.py:21
  13.3 1.3 collective-permute-start.1
  19.6 3.5 collective-permute-start.2
  23.1 1.3 collective-permute-start.3
  27.4 2.5 collective-permute-done.3
  30.0 1.3 collective-permute-start.4
  31.3 1.3 collective-permute-start.5
  35.9 50.8 %shard_map.211 = (f32[128,128]{1,0:T(8,128)}, bf16[236,48,128]{2,1,0:T(8,128)(2,1)}, bf16[236,128,48]{2,1,0:T(8,128)(2,1)}) custom-call(s32[128,16]{1,0:T(8,128)} %get-tuple-element.82.lookup, f32[236,4,128]{2,1,0:T(4,128)} %maximum_subtract_fusion.stacked), custom_call_target="tpu_custom_call" | custom-call | tf_op jit(solution)/shard_map/pallas_call | solution.py:140
  86.7 1.5 gather_fusion.2
  88.4 4.3 collective-permute-start.6
  92.7 1.3 collective-permute-start.7
  94.1 4.3 collective-permute-done.7
  98.4 3.5 collective-permute-start.8
  101.9 1.3 collective-permute-start.9
  103.5 4.2 collective-permute-done.9
  107.8 1.3 collective-permute-start.10
  109.1 1.3 collective-permute-start.11
  110.5 1.7 collective-permute-done.11
  112.3 1.5 fusion.1.term
  113.8 91.8 %shard_map.212 = f32[128,3,128]{2,1,0:T(4,128)} custom-call(s32[128,16]{1,0:T(8,128)} %get-tuple-element.82.lookup, bf16[236,48,128]{2,1,0:T(8,128)(2,1)} %get-tuple-element.21.home, bf16[236,128,48]{2,1,0:T(8,128)(2,1)} %get-tuple-element.22.away, f32[236,4,128]{2,1,0:T(4,128)} %maximum_subtract_fusion.stacked, f32[236,128]{1,0:T(8,128)} %fusion.1.term), custom_call_target="tpu_custom_call" | custom-call | tf_op jit(solution)/shard_map/pallas_call | solution.py:140
  207.1 4.6 %scatter_fusion.1 = f32[12,8,128]{2,1,0:T(8,128)S(1)} fusion(f32[12,8,128]{2,1,0:T(8,128)S(1)} %broadcast_in_dim.185, s32[128]{0:T(128)S(1)} %compare_select_fusion.2, f32[128,8,128]{2,1,0:T(8,128)S(1)} %select_maximum_fusion), kind=kCustom, calls=%fused_computation.7 | custom fusion | bytes 1573376 | tf_op jit(solution)/shard_map/scatter | solution.py:281
  211.8 4.8 %collective-permute-start.12 = (f32[1,2,8,128]{3,2,1,0:T(8,128)S(1)}, f32[1,2,8,128]{3,2,1,0:T(8,128)S(1)}, u32[]{:S(2)}, u32[]{:S(2)}) collective-permute-start(f32[1,2,8,128]{3,2,1,0:T(8,128)S(1)} %get-tuple-element.75), channel_id=1, source_target_pairs={{0,8},{8,16},{16,24},{1,9},{9,17},{17,25},{2,10},{10,18},{18,26},{... | collective-permute-start | bytes 24584 | tf_op jit(solution)/shard_map/ppermute | solution.py:21
  216.8 1.3 collective-permute-start.13
  218.1 3.5 collective-permute-start.14
  221.5 1.3 collective-permute-start.15
  222.8 1.5 collective-permute-start.16
  224.4 4.3 scatter_fusion
  228.7 1.3 collective-permute-start.17
  230.1 1.7 collective-permute-done.17
  234.3 4.3 %collective-permute-start.18 = (f32[1,3,3,4,4,128]{5,4,3,2,1,0:T(4,128)S(1)}, f32[1,3,3,4,4,128]{5,4,3,2,1,0:T(4,128)S(1)}, u32[]{:S(2)}, u32[]{:S(2)}) collective-permute-start(f32[1,3,3,4,4,128]{5,4,3,2,1,0:T(4,128)S(1)} %bitcast.81), channel_id=1, source_target_pairs={{0,8},{8,16},{16,24},{1,9},{9,17},{17,25},{2,10},{10,18},{18,26},{... | collective-permute-start | bytes 221192 | tf_op jit(solution)/shard_map/ppermute | solution.py:21
  238.6 1.3 collective-permute-start.19
  240.6 4.3 collective-permute-done.19
  245.0 4.6 %collective-permute-start.20 = (f32[5,1,3,4,4,128]{5,4,3,2,1,0:T(4,128)S(1)}, f32[5,1,3,4,4,128]{5,4,3,2,1,0:T(4,128)S(1)}, u32[]{:S(2)}, u32[]{:S(2)}) collective-permute-start(f32[5,1,3,4,4,128]{5,4,3,2,1,0:T(4,128)S(1)} %get-tuple-element.50), channel_id=1, source_target_pairs={{0,2},{2,4},{4,6},{1,3},{3,5},{5,7},{8,10},{10,12},{12,14},{9,11},... | collective-permute-start | bytes 368648 | tf_op jit(solution)/shard_map/ppermute | solution.py:21
  249.5 1.3 collective-permute-start.21
  251.9 4.4 %collective-permute-done.21 = f32[5,1,3,4,4,128]{5,4,3,2,1,0:T(4,128)S(1)} collective-permute-done((f32[5,1,3,4,4,128]{5,4,3,2,1,0:T(4,128)S(1)}, f32[5,1,3,4,4,128]{5,4,3,2,1,0:T(4,128)S(1)}, u32[]{:S(2)}, u32[]{:S(2)}) %collective-permute-start.21) | collective-permute-done | bytes 122912 | tf_op jit(solution)/shard_map/ppermute | solution.py:24
  256.4 1.3 collective-permute-start.22
  259.0 2.0 collective-permute-done.23
  262.3 51.0 %shard_map.213 = (f32[128,128]{1,0:T(8,128)}, bf16[236,48,128]{2,1,0:T(8,128)(2,1)}, bf16[236,128,48]{2,1,0:T(8,128)(2,1)}) custom-call(s32[128,16]{1,0:T(8,128)} %get-tuple-element.83.lookup, f32[236,4,128]{2,1,0:T(4,128)} %maximum_subtract_fusion.1.stacked), custom_call_target="tpu_custom_call" | custom-call | tf_op jit(solution)/shard_map/pallas_call | solution.py:140
  313.3 1.5 gather_fusion.5
  315.0 3.7 collective-permute-start.24
  320.1 4.2 collective-permute-done.25
  324.4 2.1 collective-permute-start.26
  328.1 4.2 collective-permute-done.27
  332.3 1.3 collective-permute-start.28
  333.6 1.3 collective-permute-start.29
  334.9 1.8 collective-permute-done.29
  336.9 1.5 fusion.3.term
  338.4 91.7 %shard_map.214 = f32[128,3,128]{2,1,0:T(4,128)} custom-call(s32[128,16]{1,0:T(8,128)} %get-tuple-element.83.lookup, bf16[236,48,128]{2,1,0:T(8,128)(2,1)} %get-tuple-element.24.home, bf16[236,128,48]{2,1,0:T(8,128)(2,1)} %get-tuple-element.25.away, f32[236,4,128]{2,1,0:T(4,128)} %maximum_subtract_fusion.1.stacked, f32[236,128]{1,0:T(8,128)} %fusion.3.term), custom_call_target="tpu_custom_call" | custom-call | tf_op jit(solution)/shard_map/pallas_call | solution.py:140
  (131 shorter events, 34.3 us)
Async XLA Ops:
  0.6 34.3 %copy-start = (f32[128,128]{1,0:T(8,128)S(1)}, f32[128,128]{1,0:T(8,128)}, u32[]{:S(2)}) copy-start(f32[128,128]{1,0:T(8,128)} %param.24) | copy-start | bytes 196612
  8.4 10.6 %collective-permute-start = (f32[1,3,3,4,4,128]{5,4,3,2,1,0:T(4,128)S(1)}, f32[1,3,3,4,4,128]{5,4,3,2,1,0:T(4,128)S(1)}, u32[]{:S(2)}, u32[]{:S(2)}) collective-permute-start(f32[1,3,3,4,4,128]{5,4,3,2,1,0:T(4,128)S(1)} %bitcast.79), channel_id=1, source_target_pairs={{0,8},{8,16},{16,24},{1,9},{9,17},{17,25},{2,10},{10,18},{18,26},{... | collective-permute-start | bytes 221192 | tf_op jit(solution)/shard_map/ppermute | solution.py:21
  13.3 6.2 %collective-permute-start.1 = (f32[1,3,3,4,4,128]{5,4,3,2,1,0:T(4,128)S(1)}, f32[1,3,3,4,4,128]{5,4,3,2,1,0:T(4,128)S(1)}, u32[]{:S(2)}, u32[]{:S(2)}) collective-permute-start(f32[1,3,3,4,4,128]{5,4,3,2,1,0:T(4,128)S(1)} %bitcast.78), channel_id=1, source_target_pairs={{8,0},{16,8},{24,16},{9,1},{17,9},{25,17},{10,2},{18,10},{26,18},{... | collective-permute-start | bytes 221192 | tf_op jit(solution)/shard_map/ppermute | solution.py:24
  19.6 7.8 %collective-permute-start.2 = (f32[5,1,3,4,4,128]{5,4,3,2,1,0:T(4,128)S(1)}, f32[5,1,3,4,4,128]{5,4,3,2,1,0:T(4,128)S(1)}, u32[]{:S(2)}, u32[]{:S(2)}) collective-permute-start(f32[5,1,3,4,4,128]{5,4,3,2,1,0:T(4,128)S(1)} %get-tuple-element.52), channel_id=1, source_target_pairs={{0,2},{2,4},{4,6},{1,3},{3,5},{5,7},{8,10},{10,12},{12,14},{9,11},... | collective-permute-start | bytes 368648 | tf_op jit(solution)/shard_map/ppermute | solution.py:21
  23.1 6.8 %collective-permute-start.3 = (f32[5,1,3,4,4,128]{5,4,3,2,1,0:T(4,128)S(1)}, f32[5,1,3,4,4,128]{5,4,3,2,1,0:T(4,128)S(1)}, u32[]{:S(2)}, u32[]{:S(2)}) collective-permute-start(f32[5,1,3,4,4,128]{5,4,3,2,1,0:T(4,128)S(1)} %get-tuple-element.53), channel_id=1, source_target_pairs={{2,0},{4,2},{6,4},{3,1},{5,3},{7,5},{10,8},{12,10},{14,12},{11,9},... | collective-permute-start | bytes 368648 | tf_op jit(solution)/shard_map/ppermute | solution.py:24
  30.0 3.6 collective-permute-start.4
  31.3 3.3 collective-permute-start.5
  34.9 170.6 %copy-start.1 = (f32[128,3,128]{2,0,1:T(8,128)S(1)}, f32[128,3,128]{2,0,1:T(8,128)}, u32[]{:S(2)}) copy-start(f32[128,3,128]{2,0,1:T(8,128)} %param.22) | copy-start | bytes 589828
  35.0 170.6 %copy-start.2 = (f32[128,3,128]{2,0,1:T(8,128)S(1)}, f32[128,3,128]{2,0,1:T(8,128)}, u32[]{:S(2)}) copy-start(f32[128,3,128]{2,0,1:T(8,128)} %param.23) | copy-start | bytes 589828
  88.4 5.7 %collective-permute-start.6 = (f32[1,3,3,4,128]{4,3,2,1,0:T(4,128)S(1)}, f32[1,3,3,4,128]{4,3,2,1,0:T(4,128)S(1)}, u32[]{:S(2)}, u32[]{:S(2)}) collective-permute-start(f32[1,3,3,4,128]{4,3,2,1,0:T(4,128)S(1)} %bitcast.84), channel_id=1, source_target_pairs={{0,8},{8,16},{16,24},{1,9},{9,17},{17,25},{2,10},{10,18},{18,26},{... | collective-permute-start | bytes 55304 | tf_op jit(solution)/shard_map/ppermute | solution.py:21
  92.7 5.8 %collective-permute-start.7 = (f32[1,3,3,4,128]{4,3,2,1,0:T(4,128)S(1)}, f32[1,3,3,4,128]{4,3,2,1,0:T(4,128)S(1)}, u32[]{:S(2)}, u32[]{:S(2)}) collective-permute-start(f32[1,3,3,4,128]{4,3,2,1,0:T(4,128)S(1)} %bitcast.82), channel_id=1, source_target_pairs={{8,0},{16,8},{24,16},{9,1},{17,9},{25,17},{10,2},{18,10},{26,18},{... | collective-permute-start | bytes 55304 | tf_op jit(solution)/shard_map/ppermute | solution.py:24
  98.4 5.0 %collective-permute-start.8 = (f32[5,1,3,4,128]{4,3,2,1,0:T(4,128)S(1)}, f32[5,1,3,4,128]{4,3,2,1,0:T(4,128)S(1)}, u32[]{:S(2)}, u32[]{:S(2)}) collective-permute-start(f32[5,1,3,4,128]{4,3,2,1,0:T(4,128)S(1)} %get-tuple-element.64), channel_id=1, source_target_pairs={{0,2},{2,4},{4,6},{1,3},{3,5},{5,7},{8,10},{10,12},{12,14},{9,11},... | collective-permute-start | bytes 92168 | tf_op jit(solution)/shard_map/ppermute | solution.py:21
  101.9 5.8 %collective-permute-start.9 = (f32[5,1,3,4,128]{4,3,2,1,0:T(4,128)S(1)}, f32[5,1,3,4,128]{4,3,2,1,0:T(4,128)S(1)}, u32[]{:S(2)}, u32[]{:S(2)}) collective-permute-start(f32[5,1,3,4,128]{4,3,2,1,0:T(4,128)S(1)} %get-tuple-element.65), channel_id=1, source_target_pairs={{2,0},{4,2},{6,4},{3,1},{5,3},{7,5},{10,8},{12,10},{14,12},{11,9},... | collective-permute-start | bytes 92168 | tf_op jit(solution)/shard_map/ppermute | solution.py:24
  107.8 2.7 collective-permute-start.10
  109.1 3.1 collective-permute-start.11
  211.8 17.0 %collective-permute-start.12 = (f32[1,2,8,128]{3,2,1,0:T(8,128)S(1)}, f32[1,2,8,128]{3,2,1,0:T(8,128)S(1)}, u32[]{:S(2)}, u32[]{:S(2)}) collective-permute-start(f32[1,2,8,128]{3,2,1,0:T(8,128)S(1)} %get-tuple-element.75), channel_id=1, source_target_pairs={{0,8},{8,16},{16,24},{1,9},{9,17},{17,25},{2,10},{10,18},{18,26},{... | collective-permute-start | bytes 24584 | tf_op jit(solution)/shard_map/ppermute | solution.py:21
  216.8 13.3 %collective-permute-start.13 = (f32[1,2,8,128]{3,2,1,0:T(8,128)S(1)}, f32[1,2,8,128]{3,2,1,0:T(8,128)S(1)}, u32[]{:S(2)}, u32[]{:S(2)}) collective-permute-start(f32[1,2,8,128]{3,2,1,0:T(8,128)S(1)} %get-tuple-element.74), channel_id=1, source_target_pairs={{8,0},{16,8},{24,16},{9,1},{17,9},{25,17},{10,2},{18,10},{26,18},{... | collective-permute-start | bytes 24584 | tf_op jit(solution)/shard_map/ppermute | solution.py:24
  218.1 12.0 %collective-permute-start.14 = (f32[1,2,8,128]{3,2,1,0:T(8,128)S(1)}, f32[1,2,8,128]{3,2,1,0:T(8,128)S(1)}, u32[]{:S(2)}, u32[]{:S(2)}) collective-permute-start(f32[1,2,8,128]{3,2,1,0:T(8,128)S(1)} %get-tuple-element.73), channel_id=1, source_target_pairs={{0,2},{2,4},{4,6},{1,3},{3,5},{5,7},{8,10},{10,12},{12,14},{9,11},... | collective-permute-start | bytes 24584 | tf_op jit(solution)/shard_map/ppermute | solution.py:21
  221.5 8.6 %collective-permute-start.15 = (f32[1,2,8,128]{3,2,1,0:T(8,128)S(1)}, f32[1,2,8,128]{3,2,1,0:T(8,128)S(1)}, u32[]{:S(2)}, u32[]{:S(2)}) collective-permute-start(f32[1,2,8,128]{3,2,1,0:T(8,128)S(1)} %get-tuple-element.72), channel_id=1, source_target_pairs={{2,0},{4,2},{6,4},{3,1},{5,3},{7,5},{10,8},{12,10},{14,12},{11,9},... | collective-permute-start | bytes 24584 | tf_op jit(solution)/shard_map/ppermute | solution.py:24
  222.8 7.3 %collective-permute-start.16 = (f32[1,2,8,128]{3,2,1,0:T(8,128)S(1)}, f32[1,2,8,128]{3,2,1,0:T(8,128)S(1)}, u32[]{:S(2)}, u32[]{:S(2)}) collective-permute-start(f32[1,2,8,128]{3,2,1,0:T(8,128)S(1)} %get-tuple-element.71), channel_id=1, source_target_pairs={{0,1},{2,3},{4,5},{6,7},{8,9},{10,11},{12,13},{14,15},{16,17},{18,... | collective-permute-start | bytes 24584 | tf_op jit(solution)/shard_map/ppermute | solution.py:21
  228.7 3.1 collective-permute-start.17
  234.3 6.3 %collective-permute-start.18 = (f32[1,3,3,4,4,128]{5,4,3,2,1,0:T(4,128)S(1)}, f32[1,3,3,4,4,128]{5,4,3,2,1,0:T(4,128)S(1)}, u32[]{:S(2)}, u32[]{:S(2)}) collective-permute-start(f32[1,3,3,4,4,128]{5,4,3,2,1,0:T(4,128)S(1)} %bitcast.81), channel_id=1, source_target_pairs={{0,8},{8,16},{16,24},{1,9},{9,17},{17,25},{2,10},{10,18},{18,26},{... | collective-permute-start | bytes 221192 | tf_op jit(solution)/shard_map/ppermute | solution.py:21
  238.6 6.2 %collective-permute-start.19 = (f32[1,3,3,4,4,128]{5,4,3,2,1,0:T(4,128)S(1)}, f32[1,3,3,4,4,128]{5,4,3,2,1,0:T(4,128)S(1)}, u32[]{:S(2)}, u32[]{:S(2)}) collective-permute-start(f32[1,3,3,4,4,128]{5,4,3,2,1,0:T(4,128)S(1)} %bitcast.80), channel_id=1, source_target_pairs={{8,0},{16,8},{24,16},{9,1},{17,9},{25,17},{10,2},{18,10},{26,18},{... | collective-permute-start | bytes 221192 | tf_op jit(solution)/shard_map/ppermute | solution.py:24
  245.0 7.0 %collective-permute-start.20 = (f32[5,1,3,4,4,128]{5,4,3,2,1,0:T(4,128)S(1)}, f32[5,1,3,4,4,128]{5,4,3,2,1,0:T(4,128)S(1)}, u32[]{:S(2)}, u32[]{:S(2)}) collective-permute-start(f32[5,1,3,4,4,128]{5,4,3,2,1,0:T(4,128)S(1)} %get-tuple-element.50), channel_id=1, source_target_pairs={{0,2},{2,4},{4,6},{1,3},{3,5},{5,7},{8,10},{10,12},{12,14},{9,11},... | collective-permute-start | bytes 368648 | tf_op jit(solution)/shard_map/ppermute | solution.py:21
  249.5 6.8 %collective-permute-start.21 = (f32[5,1,3,4,4,128]{5,4,3,2,1,0:T(4,128)S(1)}, f32[5,1,3,4,4,128]{5,4,3,2,1,0:T(4,128)S(1)}, u32[]{:S(2)}, u32[]{:S(2)}) collective-permute-start(f32[5,1,3,4,4,128]{5,4,3,2,1,0:T(4,128)S(1)} %get-tuple-element.51), channel_id=1, source_target_pairs={{2,0},{4,2},{6,4},{3,1},{5,3},{7,5},{10,8},{12,10},{14,12},{11,9},... | collective-permute-start | bytes 368648 | tf_op jit(solution)/shard_map/ppermute | solution.py:24
  256.4 2.6 collective-permute-start.22
  257.7 3.3 collective-permute-start.23
  315.0 5.2 %collective-permute-start.24 = (f32[1,3,3,4,128]{4,3,2,1,0:T(4,128)S(1)}, f32[1,3,3,4,128]{4,3,2,1,0:T(4,128)S(1)}, u32[]{:S(2)}, u32[]{:S(2)}) collective-permute-start(f32[1,3,3,4,128]{4,3,2,1,0:T(4,128)S(1)} %bitcast.85), channel_id=1, source_target_pairs={{0,8},{8,16},{16,24},{1,9},{9,17},{17,25},{2,10},{10,18},{18,26},{... | collective-permute-start | bytes 55304 | tf_op jit(solution)/shard_map/ppermute | solution.py:21
  318.7 5.7 %collective-permute-start.25 = (f32[1,3,3,4,128]{4,3,2,1,0:T(4,128)S(1)}, f32[1,3,3,4,128]{4,3,2,1,0:T(4,128)S(1)}, u32[]{:S(2)}, u32[]{:S(2)}) collective-permute-start(f32[1,3,3,4,128]{4,3,2,1,0:T(4,128)S(1)} %bitcast.83), channel_id=1, source_target_pairs={{8,0},{16,8},{24,16},{9,1},{17,9},{25,17},{10,2},{18,10},{26,18},{... | collective-permute-start | bytes 55304 | tf_op jit(solution)/shard_map/ppermute | solution.py:24
  324.4 3.7 collective-permute-start.26
  326.5 5.8 %collective-permute-start.27 = (f32[5,1,3,4,128]{4,3,2,1,0:T(4,128)S(1)}, f32[5,1,3,4,128]{4,3,2,1,0:T(4,128)S(1)}, u32[]{:S(2)}, u32[]{:S(2)}) collective-permute-start(f32[5,1,3,4,128]{4,3,2,1,0:T(4,128)S(1)} %get-tuple-element.63), channel_id=1, source_target_pairs={{2,0},{4,2},{6,4},{3,1},{5,3},{7,5},{10,8},{12,10},{14,12},{11,9},... | collective-permute-start | bytes 92168 | tf_op jit(solution)/shard_map/ppermute | solution.py:24
  332.3 2.6 collective-permute-start.28
  333.6 3.1 collective-permute-start.29
